TPU v7x, 32 devices: a whole 2x2x4 slice. The times are simulated.
32 devices in a mesh: area: 4 (over y, x), scen: 8 (over z, core).
Axes of the slice: x: 2, y: 2, z: 4, core: 2. Of those that a mesh axis runs over, the one named last changes fastest.
Arguments:
- load: float32 [64, 12, 8192], P('scen', None, 'area'), may hold values from -6 to 6
- start: float32 [64, 12, 8192], P('scen', None, 'area'), may hold values from -6 to 6
- multipliers: float32 [64, 12, 1024], P('scen', None, 'area'), may hold values from -4 to 4
- weights: float32 [64], P('scen'), may hold values from 0.25 to 4
- penalty: float32 [1024], P('area'), may hold values from 0.3 to 3
- inverse: bfloat16 [8192, 2048], P('area'), may hold values from -1 to 2
- ports: int32 [4, 128], replicated, may hold values from 0 to 2047
- neighbour: int32 [4, 4], replicated, may hold values from 0 to 3, as said below
- remote_port: int32 [4, 4, 32], replicated, may hold values from 0 to 127
- local_bus: int32 [4, 4, 32], replicated, may hold values from 0 to 2047
- susceptance: float32 [4, 4, 32], replicated, may hold values from 0.5 to 2
Outputs:
- solution: float32 [64, 12, 8192], P('scen', None, 'area')
- new_multipliers: float32 [64, 12, 1024], P('scen', None, 'area')
- consensus: float32 [12, 1024], P(None, 'area')
- spreads: float32 [4, 5], P('area')
Inputs may be any that keep to these rules, and one draw needn't show every extreme that they name: `neighbour`: each entry names an area other than its row's own.
All inputs are finite; a program needn't handle non-finite values.
Results may differ from a plain program's by a relative error of at most 0.012.
Values may be sent and summed in bfloat16 or wider, within the bound.
A program may use at most 64 MiB of HBM per device.

v0:
```python
import jax
import jax.numpy as jnp
from jax import lax
from jax.sharding import PartitionSpec as P

ITERS = 4


def scenario_mean(dispatch, weights):
    weighted = weights[:, None, None] * dispatch
    partial_sum = jnp.sum(weighted, axis=0)
    weight_total = jnp.sum(weights)
    cell_count = dispatch.shape[1] * dispatch.shape[2]
    square_sum = jnp.sum(weighted * dispatch)
    summed, weight_sum, squares = lax.psum((partial_sum, weight_total, square_sum), "scen")
    average = summed / weight_sum
    spread = (squares / weight_sum - jnp.sum(average * average)) / cell_count
    return (average, spread)


def shards(
    load,
    start,
    multipliers,
    weights,
    penalty,
    inverse,
    ports,
    neighbour,
    remote_port,
    local_bus,
    susceptance,
):
    scen_dev, hours, buses = start.shape
    generators = multipliers.shape[2]
    row_count = scen_dev * hours
    own_area = lax.axis_index("area")
    angles = start.reshape(row_count, buses)
    demand = load.reshape(row_count, buses)
    own_ports = ports[own_area]
    tie_buses = local_bus[own_area].reshape(-1)
    tie_weights = susceptance[own_area].reshape(-1)
    bus_ids = jnp.arange(buses, dtype=jnp.int32)
    spread_map = jnp.where(tie_buses[:, None] == bus_ids[None, :], tie_weights[:, None], 0.0)
    duals = multipliers
    average, spread = scenario_mean(start[:, :, :generators], weights)
    spread_list = [spread]
    for iteration in range(ITERS):
        offered = jnp.take(angles, own_ports, axis=1).astype(jnp.bfloat16)
        everyone = lax.all_gather(offered[None], "area", axis=0, tiled=True)
        received = everyone[neighbour[own_area][:, None], :, remote_port[own_area]]
        received = received.reshape(-1, row_count).T.astype(jnp.float32)
        inflow = jnp.dot(
            received,
            spread_map,
            precision=lax.Precision.HIGHEST,
            preferred_element_type=jnp.float32,
        )
        hedge = (penalty[None, None] * average[None] - duals).reshape(row_count, generators)
        right_side = demand + inflow
        right_side = right_side.at[:, :generators].add(hedge)
        angles = jnp.dot(
            right_side.astype(jnp.bfloat16), inverse, preferred_element_type=jnp.float32
        )
        dispatch = angles[:, :generators].reshape(scen_dev, hours, generators)
        average, spread = scenario_mean(dispatch, weights)
        duals = duals + penalty[None, None] * (dispatch - average[None])
        spread_list.append(spread)
    return (angles.reshape(scen_dev, hours, buses), duals, average, jnp.stack(spread_list)[None])


def solution(mesh):
    placed = (
        P("scen", None, "area"),
        P("scen", None, "area"),
        P("scen", None, "area"),
        P("scen"),
        P("area"),
        P("area", None),
        P(),
        P(),
        P(),
        P(),
        P(),
    )
    return jax.shard_map(
        shards,
        mesh=mesh,
        in_specs=placed,
        out_specs=(
            P("scen", None, "area"),
            P("scen", None, "area"),
            P(None, "area"),
            P("area", None),
        ),
        check_vma=False,
    )
```

profile of v0, /device:TPU:0, one launch (start us, length us, event | category | flops | bytes accessed | tf_op | source)
XLA Modules:
  0.0 240.4 jit_solution(103017015893936891)
XLA Ops:
  1.5 1.6 copy.76
  4.3 9.8 %all-gather = bf16[384,128]{1,0:T(8,128)(2,1)S(1)} all-gather(bf16[96,128]{1,0:T(8,128)(2,1)S(1)} %bitcast_convert_fusion.3), channel_id=2, replica_groups=mesh['area'=4,'scen'=8] {'area'}, dimensions={0}, use_global_device_ids=true | all-gather | bytes 122880 | tf_op jit(solution)/shard_map/all_gather | solution.py:50
  15.8 1.1 gather_fusion
  17.8 1.6 copy.75
  21.6 28.0 %all-reduce.1 = (f32[12,256]{1,0:T(8,128)S(1)}, f32[]{:T(128)}) all-reduce(f32[12,256]{1,0:T(8,128)S(1)} %get-tuple-element.70, f32[]{:T(128)} %reduce_sum.161), channel_id=1, replica_groups=mesh['area'=4,'scen'=8] {'scen'}, use_global_device_ids=true, to_apply=%region_2.0 | all-reduce | flops 3073 | bytes 24584 | tf_op jit(solution)/shard_map/psum | solution.py:15
  49.6 1.3 multiply_reduce_fusion.9
  52.2 4.9 %fusion.22 = f32[96,2048]{1,0:T(8,128)S(1)} fusion(bf16[2048,2048]{1,0:T(8,128)(2,1)} %param.26, f32[96,2048]{1,0:T(8,128)S(1)} %fusion.25), kind=kOutput, calls=%fused_computation.35 | convolution fusion | flops 805502976 | bytes 9961472 | tf_op jit(solution)/shard_map/dot_general | solution.py:62
  57.2 25.9 %psum.91 = f32[12,256]{1,0:T(8,128)S(1)} all-reduce(f32[12,256]{1,0:T(8,128)S(1)} %multiply_reduce_fusion.4), channel_id=1, replica_groups=mesh['area'=4,'scen'=8] {'scen'}, use_global_device_ids=true, to_apply=%region_6.0 | all-reduce | flops 3072 | bytes 24576 | tf_op jit(solution)/shard_map/psum | solution.py:15
  83.1 1.4 multiply_reduce_fusion.8
  85.7 8.3 %all-gather.1 = bf16[384,128]{1,0:T(8,128)(2,1)S(1)} all-gather(bf16[96,128]{1,0:T(8,128)(2,1)S(1)} %bitcast_convert_fusion.2), channel_id=3, replica_groups=mesh['area'=4,'scen'=8] {'area'}, dimensions={0}, use_global_device_ids=true | all-gather | bytes 122880 | tf_op jit(solution)/shard_map/all_gather | solution.py:50
  94.1 1.1 gather_fusion.1
  96.6 4.8 %fusion.20 = f32[96,2048]{1,0:T(8,128)S(1)} fusion(bf16[2048,2048]{1,0:T(8,128)(2,1)} %param.26, f32[96,2048]{1,0:T(8,128)S(1)} %fusion.26), kind=kOutput, calls=%fused_computation.33 | convolution fusion | flops 805502976 | bytes 9961472 | tf_op jit(solution)/shard_map/dot_general | solution.py:62
  101.6 25.9 %psum.92 = f32[12,256]{1,0:T(8,128)S(1)} all-reduce(f32[12,256]{1,0:T(8,128)S(1)} %multiply_reduce_fusion.3), channel_id=1, replica_groups=mesh['area'=4,'scen'=8] {'scen'}, use_global_device_ids=true, to_apply=%region_8.10 | all-reduce | flops 3072 | bytes 24576 | tf_op jit(solution)/shard_map/psum | solution.py:15
  127.5 1.3 multiply_reduce_fusion.7
  130.1 7.6 %all-gather.2 = bf16[384,128]{1,0:T(8,128)(2,1)S(1)} all-gather(bf16[96,128]{1,0:T(8,128)(2,1)S(1)} %bitcast_convert_fusion.1), channel_id=4, replica_groups=mesh['area'=4,'scen'=8] {'area'}, dimensions={0}, use_global_device_ids=true | all-gather | bytes 122880 | tf_op jit(solution)/shard_map/all_gather | solution.py:50
  137.8 1.1 gather_fusion.2
  140.3 4.8 %fusion.18 = f32[96,2048]{1,0:T(8,128)S(1)} fusion(bf16[2048,2048]{1,0:T(8,128)(2,1)} %param.26, f32[96,2048]{1,0:T(8,128)S(1)} %fusion.27), kind=kOutput, calls=%fused_computation.31 | convolution fusion | flops 805502976 | bytes 9961472 | tf_op jit(solution)/shard_map/dot_general | solution.py:62
  145.3 25.9 %psum.93 = f32[12,256]{1,0:T(8,128)S(1)} all-reduce(f32[12,256]{1,0:T(8,128)S(1)} %multiply_reduce_fusion.2), channel_id=1, replica_groups=mesh['area'=4,'scen'=8] {'scen'}, use_global_device_ids=true, to_apply=%region_10.12 | all-reduce | flops 3072 | bytes 24576 | tf_op jit(solution)/shard_map/psum | solution.py:15
  171.2 1.3 multiply_reduce_fusion.6
  173.8 1.0 copy.89
  174.8 1.9 gather_fusion.7
  177.5 8.9 %all-gather.3 = bf16[384,128]{1,0:T(8,128)(2,1)} all-gather(bf16[96,128]{1,0:T(8,128)(2,1)S(1)} %bitcast_convert_fusion), channel_id=5, replica_groups=mesh['area'=4,'scen'=8] {'area'}, dimensions={0}, use_global_device_ids=true | all-gather | bytes 122880 | tf_op jit(solution)/shard_map/all_gather | solution.py:50
  186.4 1.0 copy.91
  187.5 1.7 gather_fusion.3
  189.2 1.5 convolution_add_fusion
  190.7 1.5 fusion.28
  192.2 4.8 %fusion.16 = f32[96,2048]{1,0:T(8,128)S(1)} fusion(bf16[2048,2048]{1,0:T(8,128)(2,1)} %param.26, f32[96,2048]{1,0:T(8,128)S(1)} %fusion.28), kind=kOutput, calls=%fused_computation.29 | convolution fusion | flops 805502976 | bytes 9961472 | tf_op jit(solution)/shard_map/dot_general | solution.py:62
  197.3 0.8 fusion.32
  198.1 27.1 %all-reduce = (f32[12,256]{1,0:T(8,128)S(1)}, f32[]{:T(128)}, f32[]{:T(128)}, f32[]{:T(128)}, f32[]{:T(128)}, /*index=5*/f32[]{:T(128)}) all-reduce(f32[12,256]{1,0:T(8,128)S(1)} %multiply_reduce_fusion.1, f32[]{:T(128)} %get-tuple-element.69, f32[]{:T(128)} %get-tuple-element.74, ...), channel_id=1, replica_groups=mesh['area'=4,'scen'=8] {'scen'}, use_global_device_ids=true, to_apply=%region_12.14 | all-reduce | flops 3077 | bytes 24616 | tf_op jit(solution)/shard_map/psum | solution.py:15
  226.6 1.3 multiply_reduce_fusion.5
  237.9 1.2 reshape.241
  239.1 1.3 copy.92
  (91 shorter events, 17.3 us)
Async XLA Ops:
  0.6 16.3 %copy-start = (f32[4,4,32]{2,1,0:T(4,128)S(1)}, f32[4,4,32]{2,1,0:T(4,128)}, u32[]{:S(2)}) copy-start(f32[4,4,32]{2,1,0:T(4,128)} %param.31) | copy-start | bytes 6148
  0.6 19.6 %copy-start.7 = (f32[8]{0:T(128)S(1)}, f32[8]{0:T(128)}, u32[]{:S(2)}) copy-start(f32[8]{0:T(128)} %param.24) | copy-start | bytes 100
  0.7 48.9 %copy-start.5 = (f32[256]{0:T(256)S(1)}, f32[256]{0:T(256)}, u32[]{:S(2)}) copy-start(f32[256]{0:T(256)} %param.25) | copy-start | bytes 3076
  0.7 50.2 %copy-start.2 = (f32[8,12,256]{2,0,1:T(8,128)S(1)}, f32[8,12,256]{2,0,1:T(8,128)}, u32[]{:S(2)}) copy-start(f32[8,12,256]{2,0,1:T(8,128)} %param.23) | copy-start | bytes 294916
  1.4 128.6 %copy-start.11 = (pred[128]{0:T(512)(128)(4,1)}, pred[128]{0:T(512)(128)(4,1)S(1)}, u32[]{:S(2)}) copy-start(pred[128]{0:T(512)(128)(4,1)S(1)} %get-tuple-element.93) | copy-start | bytes 388
  1.4 127.8 %copy-start.12 = (s32[1024]{0:T(1024)}, s32[1024]{0:T(1024)S(1)}, u32[]{:S(2)}) copy-start(s32[1024]{0:T(1024)S(1)} %pad_clamp_fusion) | copy-start | bytes 12292
  17.0 121.9 %copy-start.9 = (f32[128]{0:T(128)}, f32[128]{0:T(128)S(1)}, u32[]{:S(2)}) copy-start(f32[128]{0:T(128)S(1)} %broadcast_in_dim.37) | copy-start | bytes 1540
  17.8 121.2 %copy-start.10 = (s32[128]{0:T(128)}, s32[128]{0:T(128)S(1)}, u32[]{:S(2)}) copy-start(s32[128]{0:T(128)S(1)} %eq.15) | copy-start | bytes 1540
  172.5 0.6 copy-start.3
  192.2 4.9 %copy-start.8 = (f32[8]{0:T(128)S(1)}, f32[8]{0:T(128)}, u32[]{:S(2)}) copy-start(f32[8]{0:T(128)} %param.24) | copy-start | bytes 100
  192.2 44.9 %copy-start.4 = (f32[12,256]{1,0:T(8,128)S(1)}, f32[12,256]{1,0:T(8,128)}, u32[]{:S(2)}) copy-start(f32[12,256]{1,0:T(8,128)} %copy-done.3) | copy-start | bytes 36868
  197.1 40.1 %copy-start.1 = (f32[96,2048]{1,0:T(8,128)}, f32[96,2048]{1,0:T(8,128)S(1)}, u32[]{:S(2)}) copy-start(f32[96,2048]{1,0:T(8,128)S(1)} %fusion.16) | copy-start | bytes 2359300
  227.9 12.5 %copy-start.6 = (f32[12,256]{1,0:T(8,128)}, f32[12,256]{1,0:T(8,128)S(1)}, u32[]{:S(2)}) copy-start(f32[12,256]{1,0:T(8,128)S(1)} %get-tuple-element.84) | copy-start | bytes 36868
where the time goes:
time: 242 us; the launch traced here: 240 us
  blocking collectives  168 us (69%)
  matrix products  23.2 us (10%)
  local copies, waits for them, and re-layouts  22.6 us (9%)
  other arithmetic  16.1 us (7%)
  between operations  11 us (5%)
    psum x5, blocking collectives, scenario_mean(): lax.psum((partial_sum, weight_total, square_sum), 'scen')  133 us
    all_gather x4, blocking collectives, shards(): everyone = lax.all_gather(offered[None], 'area', axis=0, tiled=True)  34.7 us
    dot_general x4, matrix products, shards(): jnp.dot(right_side.astype(jnp.bfloat16), inverse, preferred_element_type=...  19.4 us
    reduce_sum x5, other arithmetic, scenario_mean(): spread = (squares / weight_sum - jnp.sum(average * average)) / cell_count  6.62 us
    unnamed x30, local copies, waits for them, and re-layouts  5.9 us
    gather x4, local copies, waits for them, and re-layouts, shards(): received = everyone[neighbour[own_area][:, None], :, remote_port[own_area]]  5.11 us

commit v1 on v0

v1 whole, which is shorter than its diff:
```python
import functools

import jax
import jax.numpy as jnp
from jax import lax
from jax.experimental import pallas as pl
from jax.experimental.pallas import tpu as pltpu
from jax.sharding import PartitionSpec as P

ITERS = 4
BLOCK = 256


def split(x):
    high = x.astype(jnp.bfloat16)
    low = (x - high.astype(jnp.float32)).astype(jnp.bfloat16)
    return high, low


def dot(a, b):
    return jnp.dot(a, b, preferred_element_type=jnp.float32)


def exact(a, b):
    return jnp.dot(a, b, precision=lax.Precision.HIGHEST, preferred_element_type=jnp.float32)


def iota(shape, axis):
    return lax.broadcasted_iota(jnp.int32, shape, axis)


def kernel(
    areas,
    groups,
    load_ref,
    start_ref,
    mult_ref,
    weight_ref,
    pen_ref,
    inv_ref,
    ports_ref,
    neigh_ref,
    rport_ref,
    lbus_ref,
    susc_ref,
    sol_ref,
    newm_ref,
    cons_ref,
    spread_ref,
    inv,
    left,
    start_b,
    full,
    h,
    pick,
    sel,
    acc,
    hsub,
    duals,
    ebuf,
    pbuf,
    dma_sem,
    esend,
    erecv,
    psend,
    precv,
):
    scen, hours, buses = load_ref.shape
    gens = mult_ref.shape[2]
    nports = ports_ref.shape[1]
    slots, ties = lbus_ref.shape[1:]
    width = slots * ties
    hp = pbuf.shape[2]
    rows = scen * hp
    blocks = buses // BLOCK
    area = lax.axis_index("area")
    group = lax.axis_index("scen")

    def fetch(j):
        cols = pl.ds(pl.multiple_of(j * BLOCK, BLOCK), BLOCK)
        return pltpu.make_async_copy(inv_ref.at[:, cols], inv.at[:, cols], dma_sem.at[j])

    for j in range(blocks):
        fetch(j).start()

    barrier = pltpu.get_barrier_semaphore()
    for o in range(1, areas):
        pl.semaphore_signal(
            barrier,
            inc=1,
            device_id={"area": lax.rem(area + o, areas)},
            device_id_type=pl.DeviceIdType.MESH,
        )
    for o in range(1, groups):
        pl.semaphore_signal(
            barrier,
            inc=1,
            device_id={"scen": lax.rem(group + o, groups)},
            device_id_type=pl.DeviceIdType.MESH,
        )

    def ecopy(i, o):
        return pltpu.make_async_remote_copy(
            src_ref=ebuf.at[i, area],
            dst_ref=ebuf.at[i, area],
            send_sem=esend.at[i, o],
            recv_sem=erecv.at[i, o],
            device_id={"area": lax.rem(area + o, areas)},
            device_id_type=pl.DeviceIdType.MESH,
        )

    def pcopy(i, o):
        return pltpu.make_async_remote_copy(
            src_ref=pbuf.at[i, group],
            dst_ref=pbuf.at[i, group],
            send_sem=psend.at[i, o],
            recv_sem=precv.at[i, o],
            device_id={"scen": lax.rem(group + o, groups)},
            device_id_type=pl.DeviceIdType.MESH,
        )

    row_id = iota((hp, gens), 0)
    weight_sum = weight_ref[0]
    for s in range(1, scen):
        weight_sum = weight_sum + weight_ref[s]

    def send_mean(i, x):
        total = jnp.zeros((hp, gens), jnp.float32)
        square = jnp.zeros((hp, gens), jnp.float32)
        for s in range(scen):
            part = x[s * hp : (s + 1) * hp, :]
            weighted = weight_ref[s] * part
            total = total + weighted
            square = square + weighted * part
        square = jnp.sum(square, axis=0, keepdims=True)
        total = jnp.where(row_id == hours, weight_sum, total)
        total = jnp.where(row_id == hours + 1, square, total)
        pbuf[i, group] = total
        for o in range(1, groups):
            pcopy(i, o).start()

    def get_mean(i):
        for o in range(1, groups):
            pcopy(i, o).wait_recv()
        total = pbuf[i, 0]
        for g in range(1, groups):
            total = total + pbuf[i, g]
        weights = total[hours : hours + 1, :]
        average = jnp.where(row_id < hours, total / weights, 0.0)
        squares = jnp.sum(total[hours + 1 : hours + 2, :])
        spread = (squares / jnp.max(weights) - jnp.sum(average * average)) / (hours * gens)
        return average, spread

    def send_ports(i, values):
        ebuf[i, area] = values.astype(jnp.bfloat16)
        for o in range(1, areas):
            ecopy(i, o).start()

    pick[...] = jnp.where(
        iota((buses, nports), 0) == ports_ref[pl.ds(area, 1), :], 1.0, 0.0
    ).astype(jnp.bfloat16)
    pad = jnp.zeros((hp - hours, buses), jnp.float32)
    for s in range(scen):
        start_b[s * hp : (s + 1) * hp, :] = jnp.concatenate(
            (start_ref[s], pad), axis=0
        ).astype(jnp.bfloat16)
    gpad = jnp.zeros((hp - hours, gens), jnp.float32)
    dispatch = jnp.concatenate(
        [
            piece
            for s in range(scen)
            for piece in (jnp.concatenate((start_ref[s, :, :gens], gpad), axis=0),)
        ],
        axis=0,
    )
    offered = dot(start_b[...], pick[...])
    pl.semaphore_wait(barrier, areas + groups - 2)
    send_ports(0, offered)
    send_mean(0, dispatch)

    def to_row(x):
        spread_out = exact(x, jnp.where(iota((ties, width), 1) % ties == iota((ties, width), 0), 1.0, 0.0))
        mine = iota((slots, width), 1) // ties == iota((slots, width), 0)
        return jnp.sum(jnp.where(mine, spread_out, 0.0), axis=0, keepdims=True)

    susc = to_row(susc_ref[area])
    rport = to_row(rport_ref[area].astype(jnp.float32))
    neigh = exact(
        neigh_ref[pl.ds(area, 1), :].astype(jnp.float32),
        jnp.where(iota((slots, width), 1) // ties == iota((slots, width), 0), 1.0, 0.0),
    )
    code = neigh * nports + rport
    sel[...] = jnp.where(
        iota((areas * nports, width), 0).astype(jnp.float32) == code, 1.0, 0.0
    ).astype(jnp.bfloat16)
    stretched = exact(
        jnp.where(iota((width, slots), 0) // ties == iota((width, slots), 1), 1.0, 0.0),
        lbus_ref[area].astype(jnp.float32),
    )
    mine = iota((width, ties), 0) % ties == iota((width, ties), 1)
    bus_col = jnp.sum(jnp.where(mine, stretched, 0.0), axis=1, keepdims=True)
    left[rows:, :] = jnp.where(
        iota((width, buses), 1).astype(jnp.float32) == bus_col, 1.0, 0.0
    ).astype(jnp.bfloat16)
    for s in range(scen):
        left[s * hp : (s + 1) * hp, :] = jnp.concatenate((load_ref[s], pad), axis=0).astype(
            jnp.bfloat16
        )
        duals[s * hp : (s + 1) * hp, :] = jnp.concatenate((mult_ref[s], gpad), axis=0)

    acc[...] = jnp.zeros_like(acc)

    def column_block(j, carry):
        fetch(j).wait()
        cols = pl.ds(pl.multiple_of(j * BLOCK, BLOCK), BLOCK)
        product = dot(left[...], inv[:, cols])
        own = product[:rows]
        full[:, cols] = own
        h[:width, cols] = product[rows:].astype(jnp.bfloat16)
        h[width:, cols] = inv[:gens, cols]
        high, low = split(own)
        stack = jnp.concatenate((high, low, h[:, cols]), axis=0)
        acc[...] += dot(stack, pick[cols, :])
        return carry

    lax.fori_loop(0, blocks, column_block, 0)

    base = jnp.concatenate((full[:, :gens], acc[:rows] + acc[rows : 2 * rows]), axis=1)
    hsub[...] = jnp.concatenate(
        (h[:, :gens], acc[2 * rows :].astype(jnp.bfloat16)), axis=1
    )
    pen = pen_ref[...]

    def gather(i, average):
        for o in range(1, areas):
            ecopy(i, o).wait_recv()
        received = dot(ebuf[i, 0], sel[:nports, :])
        for b in range(1, areas):
            received = received + dot(ebuf[i, b], sel[b * nports : (b + 1) * nports, :])
        hedge = jnp.concatenate([pen * average] * scen, axis=0) - duals[...]
        return jnp.concatenate((received * susc, hedge), axis=1)

    spreads = []
    average, spread = get_mean(0)
    spreads.append(spread)
    for i in range(ITERS):
        source = gather(i, average)
        high, low = split(source)
        update = base + dot(high, hsub[...]) + dot(low, hsub[...])
        if i < ITERS - 1:
            send_ports(i + 1, update[:, gens:])
        dispatch = update[:, :gens]
        send_mean(i + 1, dispatch)
        if i == ITERS - 1:
            for s in range(scen):
                sol_ref[s, :, :gens] = dispatch[s * hp : s * hp + hours]

            for j in range(gens // BLOCK, blocks):
                cols = slice(j * BLOCK, (j + 1) * BLOCK)
                out = full[:, cols] + dot(high, h[:, cols]) + dot(low, h[:, cols])
                for s in range(scen):
                    sol_ref[s, :, cols] = out[s * hp : s * hp + hours]
        average, spread = get_mean(i + 1)
        spreads.append(spread)
        duals[...] = duals[...] + pen * (dispatch - jnp.concatenate([average] * scen, axis=0))

    for s in range(scen):
        newm_ref[s] = duals[s * hp : s * hp + hours, :]
    cons_ref[...] = average[:hours]
    lane = iota(spread_ref.shape, 1)
    line = jnp.zeros(spread_ref.shape, jnp.float32)
    for i, spread in enumerate(spreads):
        line = jnp.where(lane == i, spread, line)
    spread_ref[...] = line

    for i in range(ITERS):
        for o in range(1, areas):
            ecopy(i, o).wait_send()
    for i in range(ITERS + 1):
        for o in range(1, groups):
            pcopy(i, o).wait_send()


def shards(areas, groups, load, start, multipliers, weights, penalty, inverse, *tables):
    scen, hours, buses = load.shape
    gens = multipliers.shape[2]
    ports, _, _, local_bus, _ = tables
    nports = ports.shape[1]
    width = local_bus.shape[1] * local_bus.shape[2]
    hp = -(-(hours + 2) // 16) * 16
    rows = scen * hp
    inner = width + gens
    bf, f32 = jnp.bfloat16, jnp.float32
    vmem = pl.BlockSpec(memory_space=pltpu.VMEM)
    dma = pltpu.SemaphoreType.DMA
    return pl.pallas_call(
        functools.partial(kernel, areas, groups),
        out_shape=(
            jax.ShapeDtypeStruct(load.shape, f32),
            jax.ShapeDtypeStruct(multipliers.shape, f32),
            jax.ShapeDtypeStruct((hours, gens), f32),
            jax.ShapeDtypeStruct((1, ITERS + 1), f32),
        ),
        in_specs=[
            vmem,
            vmem,
            vmem,
            pl.BlockSpec(memory_space=pltpu.SMEM),
            vmem,
            pl.BlockSpec(memory_space=pl.ANY),
        ]
        + [vmem] * 5,
        out_specs=(vmem,) * 4,
        scratch_shapes=[
            pltpu.VMEM((buses, buses), bf),
            pltpu.VMEM((rows + width, buses), bf),
            pltpu.VMEM((rows, buses), bf),
            pltpu.VMEM((rows, buses), f32),
            pltpu.VMEM((inner, buses), bf),
            pltpu.VMEM((buses, nports), bf),
            pltpu.VMEM((areas * nports, width), bf),
            pltpu.VMEM((2 * rows + inner, nports), f32),
            pltpu.VMEM((inner, gens + nports), bf),
            pltpu.VMEM((rows, gens), f32),
            pltpu.VMEM((ITERS, areas, rows, nports), bf),
            pltpu.VMEM((ITERS + 1, groups, hp, gens), f32),
            dma((buses // BLOCK,)),
            dma((ITERS, areas)),
            dma((ITERS, areas)),
            dma((ITERS + 1, groups)),
            dma((ITERS + 1, groups)),
        ],
        compiler_params=pltpu.CompilerParams(collective_id=0, has_side_effects=True),
        name="hedging",
    )(load, start, multipliers, weights, penalty.reshape(1, gens), inverse, *tables)


def solution(mesh):
    placed = (
        P("scen", None, "area"),
        P("scen", None, "area"),
        P("scen", None, "area"),
        P("scen"),
        P("area"),
        P("area", None),
        P(),
        P(),
        P(),
        P(),
        P(),
    )
    return jax.shard_map(
        functools.partial(shards, mesh.shape["area"], mesh.shape["scen"]),
        mesh=mesh,
        in_specs=placed,
        out_specs=(
            P("scen", None, "area"),
            P("scen", None, "area"),
            P(None, "area"),
            P("area", None),
        ),
        check_vma=False,
    )
```

time: 242 us -> 50.9 us (0.21)
  blocking collectives: 168 us -> 0 us
  Pallas kernels: 0 us -> 36.4 us
  matrix products: 23.2 us -> 0 us
  other arithmetic: 16.1 us -> 0 us
  between operations: 11 us -> 0.64 us
  local copies, waits for them, and re-layouts: 22.6 us -> 13.4 us
    psum x5 -> x0, blocking collectives: 133 us -> none  [scenario_mean(): lax.psum((partial_sum, weight_total, square_sum), 'scen')]
    pallas_call x0 -> x1, Pallas kernels: none -> 36.4 us  [shards(): pl.pallas_call(functools.partial(kernel, areas, groups), out_shape=(jax.S...]
    all_gather x4 -> x0, blocking collectives: 34.7 us -> none  [shards(): everyone = lax.all_gather(offered[None], 'area', axis=0, tiled=True)]
    dot_general x8 -> x0, matrix products: 23.2 us -> none  [the longest x4 19.4 us: shards(): jnp.dot(right_side.astype(jnp.bfloat16), inverse, preferred_element_type=...]
    gather x12 -> x0, local copies, waits for them, and re-layouts: 9.52 us -> none  [the longest x4 5.11 us: shards(): received = everyone[neighbour[own_area][:, None], :, remote_port[own_area]]]
    reduce_sum x12 -> x0, other arithmetic: 9.03 us -> none  [the longest x5 6.62 us: scenario_mean(): spread = (squares / weight_sum - jnp.sum(average * average)) / cell_count]
    pallas_call x0 -> x2, local copies, waits for them, and re-layouts: none -> 4.17 us  [shards(): pl.pallas_call(functools.partial(kernel, areas, groups), out_shape=(jax.S...]
    unnamed x30 -> x5, local copies, waits for them, and re-layouts: 5.9 us -> 9.28 us
where the time goes in v1:
time: 50.9 us; the launch traced here: 50.5 us
  Pallas kernels  36.4 us (72%)
  local copies, waits for them, and re-layouts  13.4 us (26%)
  between operations  0.64 us (1%)
    pallas_call x1, Pallas kernels, shards(): pl.pallas_call(functools.partial(kernel, areas, groups), out_shape=(jax.S...  36.4 us
    unnamed x5, local copies, waits for them, and re-layouts  9.28 us
    pallas_call x2, local copies, waits for them, and re-layouts, shards(): pl.pallas_call(functools.partial(kernel, areas, groups), out_shape=(jax.S...  4.17 us

profile of v1, /device:TPU:0, one launch (start us, length us, event | category | flops | bytes accessed | tf_op | source)
XLA Modules:
  0.0 50.5 jit_solution(16754983280892833253)
XLA Ops:
  0.6 1.6 %copy.17.mult_ref = f32[8,12,256]{2,1,0:T(8,128)} copy(f32[8,12,256]{2,0,1:T(8,128)} %param.13) | data formatting | bytes 196608 | tf_op args[2]
  2.2 2.6 %copy.15.load_ref = f32[8,12,2048]{2,1,0:T(8,128)} copy(f32[8,12,2048]{2,0,1:T(8,128)} %param.11) | data formatting | bytes 1572864 | tf_op args[0]
  4.8 2.6 %copy.16.start_ref = f32[8,12,2048]{2,1,0:T(8,128)} copy(f32[8,12,2048]{2,0,1:T(8,128)} %param.12) | data formatting | bytes 1572864 | tf_op args[1]
  7.4 36.4 %hedging.1 = (f32[8,12,2048]{2,1,0:T(8,128)}, f32[8,12,256]{2,1,0:T(8,128)}, f32[12,256]{1,0:T(8,128)}, f32[1,5]{1,0:T(1,128)}) custom-call(f32[8,12,2048]{2,1,0:T(8,128)} %copy.15.load_ref, f32[8,12,2048]{2,1,0:T(8,128)} %copy.16.start_ref, f32[8,12,256]{2,1,0:T(8,128)} %copy.17.mult_ref, f32[8]{0:T(128)} %weight_ref.1, f32[1,256]{1,0:T(1,128)} %bitcast.1, ...), custom_call_target="tpu_custom_call" | custom-call | tf_op jit(solution)/shard_map/hedging/pallas_call | solution.py:296
  43.9 2.6 %copy.18 = f32[8,12,2048]{2,0,1:T(8,128)} copy(f32[8,12,2048]{2,1,0:T(8,128)} %get-tuple-element.4) | data formatting | bytes 1572864 | tf_op jit(solution)/shard_map/hedging/pallas_call | solution.py:296
  46.4 1.6 %copy.19 = f32[8,12,256]{2,0,1:T(8,128)} copy(f32[8,12,256]{2,1,0:T(8,128)} %get-tuple-element.5) | data formatting | bytes 196608 | tf_op jit(solution)/shard_map/hedging/pallas_call | solution.py:296
  48.0 1.3 %copy.22 = f32[12,256]{1,0:T(8,128)} copy(f32[12,256]{1,0:T(8,128)} %get-tuple-element.14) | data formatting | bytes 24576
  49.3 1.2 %copy.23 = f32[1,5]{1,0:T(1,128)} copy(f32[1,5]{1,0:T(1,128)} %get-tuple-element.15) | data formatting | bytes 40

commit v2 on v1

--- a/solution.py
+++ b/solution.py
@@ -49,7 +49,6 @@
     spread_ref,
     inv,
     left,
-    start_b,
     full,
     h,
     pick,
@@ -65,13 +64,14 @@
     psend,
     precv,
 ):
-    scen, hours, buses = load_ref.shape
-    gens = mult_ref.shape[2]
+    rows, buses = load_ref.shape
+    gens = mult_ref.shape[1]
+    scen = weight_ref.shape[0]
+    hours = rows // scen
     nports = ports_ref.shape[1]
     slots, ties = lbus_ref.shape[1:]
     width = slots * ties
     hp = pbuf.shape[2]
-    rows = scen * hp
     blocks = buses // BLOCK
     area = lax.axis_index("area")
     group = lax.axis_index("scen")
@@ -119,23 +119,23 @@
             device_id_type=pl.DeviceIdType.MESH,
         )
 
-    row_id = iota((hp, gens), 0)
-    weight_sum = weight_ref[0]
-    for s in range(1, scen):
-        weight_sum = weight_sum + weight_ref[s]
+    seat = iota((scen, gens), 0)
+    weights = jnp.zeros((scen, gens), jnp.float32)
+    for s in range(scen):
+        weights = jnp.where(seat == s, weight_ref[s], weights)
+    weight_sum = jnp.sum(weights, axis=0, keepdims=True)
+
+    def over_scenarios(x):
+        return jnp.broadcast_to(x[:, None, :], (hours, scen, gens)).reshape(rows, gens)
 
     def send_mean(i, x):
-        total = jnp.zeros((hp, gens), jnp.float32)
-        square = jnp.zeros((hp, gens), jnp.float32)
-        for s in range(scen):
-            part = x[s * hp : (s + 1) * hp, :]
-            weighted = weight_ref[s] * part
-            total = total + weighted
-            square = square + weighted * part
-        square = jnp.sum(square, axis=0, keepdims=True)
-        total = jnp.where(row_id == hours, weight_sum, total)
-        total = jnp.where(row_id == hours + 1, square, total)
-        pbuf[i, group] = total
+        weighted = weights[None] * x.reshape(hours, scen, gens)
+        square = jnp.sum(weighted * x.reshape(hours, scen, gens), axis=(0, 1))[None]
+        pbuf[i, group, :hours, :] = jnp.sum(weighted, axis=1)
+        pbuf[i, group, hours : hours + 1, :] = weight_sum
+        pbuf[i, group, hours + 1 : hours + 2, :] = square
+        if hp > hours + 2:
+            pbuf[i, group, hours + 2 :, :] = jnp.zeros((hp - hours - 2, gens), jnp.float32)
         for o in range(1, groups):
             pcopy(i, o).start()
 
@@ -145,10 +145,10 @@
         total = pbuf[i, 0]
         for g in range(1, groups):
             total = total + pbuf[i, g]
-        weights = total[hours : hours + 1, :]
-        average = jnp.where(row_id < hours, total / weights, 0.0)
+        everything = total[hours : hours + 1, :]
+        average = total[:hours] / everything
         squares = jnp.sum(total[hours + 1 : hours + 2, :])
-        spread = (squares / jnp.max(weights) - jnp.sum(average * average)) / (hours * gens)
+        spread = (squares / jnp.max(everything) - jnp.sum(average * average)) / (hours * gens)
         return average, spread
 
     def send_ports(i, values):
@@ -159,21 +159,9 @@
     pick[...] = jnp.where(
         iota((buses, nports), 0) == ports_ref[pl.ds(area, 1), :], 1.0, 0.0
     ).astype(jnp.bfloat16)
-    pad = jnp.zeros((hp - hours, buses), jnp.float32)
-    for s in range(scen):
-        start_b[s * hp : (s + 1) * hp, :] = jnp.concatenate(
-            (start_ref[s], pad), axis=0
-        ).astype(jnp.bfloat16)
-    gpad = jnp.zeros((hp - hours, gens), jnp.float32)
-    dispatch = jnp.concatenate(
-        [
-            piece
-            for s in range(scen)
-            for piece in (jnp.concatenate((start_ref[s, :, :gens], gpad), axis=0),)
-        ],
-        axis=0,
-    )
-    offered = dot(start_b[...], pick[...])
+    start_b = start_ref[...].astype(jnp.bfloat16)
+    dispatch = start_ref[:, :gens]
+    offered = dot(start_b, pick[...])
     pl.semaphore_wait(barrier, areas + groups - 2)
     send_ports(0, offered)
     send_mean(0, dispatch)
@@ -202,11 +190,8 @@
     left[rows:, :] = jnp.where(
         iota((width, buses), 1).astype(jnp.float32) == bus_col, 1.0, 0.0
     ).astype(jnp.bfloat16)
-    for s in range(scen):
-        left[s * hp : (s + 1) * hp, :] = jnp.concatenate((load_ref[s], pad), axis=0).astype(
-            jnp.bfloat16
-        )
-        duals[s * hp : (s + 1) * hp, :] = jnp.concatenate((mult_ref[s], gpad), axis=0)
+    left[:rows, :] = load_ref[...].astype(jnp.bfloat16)
+    duals[...] = mult_ref[...]
 
     acc[...] = jnp.zeros_like(acc)
 
@@ -237,7 +222,7 @@
         received = dot(ebuf[i, 0], sel[:nports, :])
         for b in range(1, areas):
             received = received + dot(ebuf[i, b], sel[b * nports : (b + 1) * nports, :])
-        hedge = jnp.concatenate([pen * average] * scen, axis=0) - duals[...]
+        hedge = over_scenarios(pen * average) - duals[...]
         return jnp.concatenate((received * susc, hedge), axis=1)
 
     spreads = []
@@ -252,21 +237,16 @@
         dispatch = update[:, :gens]
         send_mean(i + 1, dispatch)
         if i == ITERS - 1:
-            for s in range(scen):
-                sol_ref[s, :, :gens] = dispatch[s * hp : s * hp + hours]
-
+            sol_ref[:, :gens] = dispatch
             for j in range(gens // BLOCK, blocks):
                 cols = slice(j * BLOCK, (j + 1) * BLOCK)
-                out = full[:, cols] + dot(high, h[:, cols]) + dot(low, h[:, cols])
-                for s in range(scen):
-                    sol_ref[s, :, cols] = out[s * hp : s * hp + hours]
+                sol_ref[:, cols] = full[:, cols] + dot(high, h[:, cols]) + dot(low, h[:, cols])
         average, spread = get_mean(i + 1)
         spreads.append(spread)
-        duals[...] = duals[...] + pen * (dispatch - jnp.concatenate([average] * scen, axis=0))
-
-    for s in range(scen):
-        newm_ref[s] = duals[s * hp : s * hp + hours, :]
-    cons_ref[...] = average[:hours]
+        duals[...] = duals[...] + pen * (dispatch - over_scenarios(average))
+
+    newm_ref[...] = duals[...]
+    cons_ref[...] = average
     lane = iota(spread_ref.shape, 1)
     line = jnp.zeros(spread_ref.shape, jnp.float32)
     for i, spread in enumerate(spreads):
@@ -281,19 +261,33 @@
             pcopy(i, o).wait_send()
 
 
+def store(*refs):
+    count = (len(refs) - 1) // 2
+    copies = [
+        pltpu.make_async_copy(refs[i], refs[count + i], refs[-1].at[i]) for i in range(count)
+    ]
+    for copy in copies:
+        copy.start()
+    for copy in copies:
+        copy.wait()
+
+
 def shards(areas, groups, load, start, multipliers, weights, penalty, inverse, *tables):
     scen, hours, buses = load.shape
     gens = multipliers.shape[2]
+    rows = scen * hours
+    load, start, multipliers = (
+        x.transpose(1, 0, 2).reshape(rows, -1) for x in (load, start, multipliers)
+    )
     ports, _, _, local_bus, _ = tables
     nports = ports.shape[1]
     width = local_bus.shape[1] * local_bus.shape[2]
-    hp = -(-(hours + 2) // 16) * 16
-    rows = scen * hp
+    hp = -(-(hours + 2) // 8) * 8
     inner = width + gens
     bf, f32 = jnp.bfloat16, jnp.float32
     vmem = pl.BlockSpec(memory_space=pltpu.VMEM)
     dma = pltpu.SemaphoreType.DMA
-    return pl.pallas_call(
+    results = pl.pallas_call(
         functools.partial(kernel, areas, groups),
         out_shape=(
             jax.ShapeDtypeStruct(load.shape, f32),
@@ -314,7 +308,6 @@
         scratch_shapes=[
             pltpu.VMEM((buses, buses), bf),
             pltpu.VMEM((rows + width, buses), bf),
-            pltpu.VMEM((rows, buses), bf),
             pltpu.VMEM((rows, buses), f32),
             pltpu.VMEM((inner, buses), bf),
             pltpu.VMEM((buses, nports), bf),
@@ -333,6 +326,18 @@
         compiler_params=pltpu.CompilerParams(collective_id=0, has_side_effects=True),
         name="hedging",
     )(load, start, multipliers, weights, penalty.reshape(1, gens), inverse, *tables)
+    solved, duals, average, spread = pl.pallas_call(
+        store,
+        out_shape=tuple(jax.ShapeDtypeStruct(x.shape, x.dtype) for x in results),
+        in_specs=[vmem] * 4,
+        out_specs=(pl.BlockSpec(memory_space=pl.ANY),) * 4,
+        scratch_shapes=[dma((4,))],
+        name="store",
+    )(*results)
+    solved, duals = (
+        x.reshape(hours, scen, -1).transpose(1, 0, 2) for x in (solved, duals)
+    )
+    return solved, duals, average, spread
 
 
 def solution(mesh):

time: 50.9 us -> 38.5 us (0.76)
  local copies, waits for them, and re-layouts: 13.4 us -> 0 us
  Pallas kernels: 36.4 us -> 37.7 us
    unnamed x5 -> x0, local copies, waits for them, and re-layouts: 9.28 us -> none
    pallas_call x2 -> x0, local copies, waits for them, and re-layouts: 4.17 us -> none  [shards(): pl.pallas_call(functools.partial(kernel, areas, groups), out_shape=(jax.S...]
    pallas_call x0 -> x1, Pallas kernels: none -> 2.13 us  [shards(): pl.pallas_call(store, out_shape=tuple((jax.ShapeDtypeStruct(x.shape, x.dt...]
    pallas_call x1, Pallas kernels: 36.4 us -> 35.6 us  [shards(): pl.pallas_call(functools.partial(kernel, areas, groups), out_shape=(jax.S...]
where the time goes in v2:
time: 38.5 us; the launch traced here: 38.3 us
  Pallas kernels  37.7 us (98%)
  between operations  0.64 us (2%)
    pallas_call x1, Pallas kernels, shards(): pl.pallas_call(functools.partial(kernel, areas, groups), out_shape=(jax.S...  35.6 us
    pallas_call x1, Pallas kernels, shards(): pl.pallas_call(store, out_shape=tuple((jax.ShapeDtypeStruct(x.shape, x.dt...  2.13 us

profile of v2, /device:TPU:0, one launch (start us, length us, event | category | flops | bytes accessed | tf_op | source)
XLA Modules:
  0.0 38.3 jit_solution(13533803160416842693)
XLA Ops:
  0.6 35.6 %hedging.1 = (f32[96,2048]{1,0:T(8,128)}, f32[96,256]{1,0:T(8,128)}, f32[12,256]{1,0:T(8,128)}, f32[1,5]{1,0:T(1,128)}) custom-call(f32[96,2048]{1,0:T(8,128)} %bitcast.16, f32[96,2048]{1,0:T(8,128)} %bitcast.17, f32[96,256]{1,0:T(8,128)} %bitcast.18, f32[8]{0:T(128)} %weight_ref.1, f32[1,256]{1,0:T(1,128)} %bitcast.19, bf16[2048,2048]{1,0:T(8,128)(2,1)} %inv_ref.1, ...), custom_call_target="tpu_custom_call" | custom-call | tf_op jit(solution)/shard_map/hedging/pallas_call | solution.py:290
  36.2 2.1 %store.1 = (f32[96,2048]{1,0:T(8,128)}, f32[96,256]{1,0:T(8,128)}, f32[12,256]{1,0:T(8,128)}, f32[1,5]{1,0:T(1,128)}) custom-call(f32[96,2048]{1,0:T(8,128)} %get-tuple-element.12.refs_0_, f32[96,256]{1,0:T(8,128)} %get-tuple-element.13.refs_1_, f32[12,256]{1,0:T(8,128)} %get-tuple-element.14.refs_2_, f32[1,5]{1,0:T(1,128)} %get-tuple-element.15.refs_3_), custom_call_target="tpu_custom_call" | custom-call | tf_op jit(solution)/shard_map/store/pallas_call | solution.py:329

commit v3 on v2

--- a/solution.py
+++ b/solution.py
@@ -32,8 +32,8 @@
 def kernel(
     areas,
     groups,
-    load_ref,
-    start_ref,
+    load_hbm,
+    start_hbm,
     mult_ref,
     weight_ref,
     pen_ref,
@@ -48,6 +48,8 @@
     cons_ref,
     spread_ref,
     inv,
+    load_ref,
+    start_ref,
     left,
     full,
     h,
@@ -58,11 +60,15 @@
     duals,
     ebuf,
     pbuf,
+    qbuf,
     dma_sem,
+    in_sem,
     esend,
     erecv,
     psend,
     precv,
+    qsend,
+    qrecv,
 ):
     rows, buses = load_ref.shape
     gens = mult_ref.shape[1]
@@ -80,6 +86,10 @@
         cols = pl.ds(pl.multiple_of(j * BLOCK, BLOCK), BLOCK)
         return pltpu.make_async_copy(inv_ref.at[:, cols], inv.at[:, cols], dma_sem.at[j])
 
+    load_in = pltpu.make_async_copy(load_hbm, load_ref, in_sem.at[0])
+    start_in = pltpu.make_async_copy(start_hbm, start_ref, in_sem.at[1])
+    start_in.start()
+    load_in.start()
     for j in range(blocks):
         fetch(j).start()
 
@@ -100,9 +110,12 @@
         )
 
     def ecopy(i, o):
+        first = rows if i == ITERS else 0
+        count = (rows if i == 0 else rows + hp) - first
+        part = ebuf.at[i, area, pl.ds(first, count)]
         return pltpu.make_async_remote_copy(
-            src_ref=ebuf.at[i, area],
-            dst_ref=ebuf.at[i, area],
+            src_ref=part,
+            dst_ref=part,
             send_sem=esend.at[i, o],
             recv_sem=erecv.at[i, o],
             device_id={"area": lax.rem(area + o, areas)},
@@ -119,52 +132,68 @@
             device_id_type=pl.DeviceIdType.MESH,
         )
 
-    seat = iota((scen, gens), 0)
-    weights = jnp.zeros((scen, gens), jnp.float32)
+    def qcopy(o):
+        return pltpu.make_async_remote_copy(
+            src_ref=qbuf.at[group],
+            dst_ref=qbuf.at[group],
+            send_sem=qsend.at[o],
+            recv_sem=qrecv.at[o],
+            device_id={"scen": lax.rem(group + o, groups)},
+            device_id_type=pl.DeviceIdType.MESH,
+        )
+
+    inside = gens + nports
+    seat = iota((scen, inside), 0)
+    weights = jnp.zeros((scen, inside), jnp.float32)
     for s in range(scen):
         weights = jnp.where(seat == s, weight_ref[s], weights)
     weight_sum = jnp.sum(weights, axis=0, keepdims=True)
+    row_id = iota((hp, inside), 0)
 
     def over_scenarios(x):
-        return jnp.broadcast_to(x[:, None, :], (hours, scen, gens)).reshape(rows, gens)
-
-    def send_mean(i, x):
-        weighted = weights[None] * x.reshape(hours, scen, gens)
-        square = jnp.sum(weighted * x.reshape(hours, scen, gens), axis=(0, 1))[None]
-        pbuf[i, group, :hours, :] = jnp.sum(weighted, axis=1)
-        pbuf[i, group, hours : hours + 1, :] = weight_sum
-        pbuf[i, group, hours + 1 : hours + 2, :] = square
-        if hp > hours + 2:
-            pbuf[i, group, hours + 2 :, :] = jnp.zeros((hp - hours - 2, gens), jnp.float32)
+        return jnp.broadcast_to(x[:hours, None, :], (hours, scen, gens)).reshape(rows, gens)
+
+    def send_sums(i, x):
+        sums = jnp.sum(weights[None] * x.reshape(hours, scen, inside), axis=1)
+        sums = jnp.concatenate((sums, jnp.zeros((hp - hours, inside), jnp.float32)), axis=0)
+        if i == 0:
+            rest = weight_sum
+            for r in range(hours, hours + 3):
+                piece = rest.astype(jnp.bfloat16).astype(jnp.float32)
+                sums = jnp.where(row_id == r, piece, sums)
+                rest = rest - piece
+        pbuf[i, group] = sums.astype(jnp.bfloat16)
         for o in range(1, groups):
             pcopy(i, o).start()
 
-    def get_mean(i):
+    def get_sums(i):
         for o in range(1, groups):
             pcopy(i, o).wait_recv()
-        total = pbuf[i, 0]
+        total = pbuf[i, 0].astype(jnp.float32)
         for g in range(1, groups):
-            total = total + pbuf[i, g]
-        everything = total[hours : hours + 1, :]
-        average = total[:hours] / everything
-        squares = jnp.sum(total[hours + 1 : hours + 2, :])
-        spread = (squares / jnp.max(everything) - jnp.sum(average * average)) / (hours * gens)
-        return average, spread
-
-    def send_ports(i, values):
-        ebuf[i, area] = values.astype(jnp.bfloat16)
+            total = total + pbuf[i, g].astype(jnp.float32)
+        return total
+
+    def squares(x, center):
+        off = x - over_scenarios(center)
+        off = off.reshape(hours, scen, gens)
+        return jnp.sum(weights[None, :, :gens] * off * off)
+
+    def send_exchange(i):
         for o in range(1, areas):
             ecopy(i, o).start()
 
     pick[...] = jnp.where(
         iota((buses, nports), 0) == ports_ref[pl.ds(area, 1), :], 1.0, 0.0
     ).astype(jnp.bfloat16)
+    start_in.wait()
     start_b = start_ref[...].astype(jnp.bfloat16)
     dispatch = start_ref[:, :gens]
     offered = dot(start_b, pick[...])
     pl.semaphore_wait(barrier, areas + groups - 2)
-    send_ports(0, offered)
-    send_mean(0, dispatch)
+    ebuf[0, area, :rows, :] = offered.astype(jnp.bfloat16)
+    send_exchange(0)
+    send_sums(0, jnp.concatenate((dispatch, offered), axis=1))
 
     def to_row(x):
         spread_out = exact(x, jnp.where(iota((ties, width), 1) % ties == iota((ties, width), 0), 1.0, 0.0))
@@ -190,8 +219,8 @@
     left[rows:, :] = jnp.where(
         iota((width, buses), 1).astype(jnp.float32) == bus_col, 1.0, 0.0
     ).astype(jnp.bfloat16)
+    load_in.wait()
     left[:rows, :] = load_ref[...].astype(jnp.bfloat16)
-    duals[...] = mult_ref[...]
 
     acc[...] = jnp.zeros_like(acc)
 
@@ -216,49 +245,94 @@
     )
     pen = pen_ref[...]
 
-    def gather(i, average):
+    def apply(source):
+        high, low = split(source)
+        return dot(high, hsub[...]) + dot(low, hsub[...])
+
+    high, low = split(mult_ref[...])
+    still = base - dot(high, hsub[width:, :]) - dot(low, hsub[width:, :])
+    send_sums(1, still)
+    total = get_sums(0)
+    everything = total[hours : hours + 1, :]
+    for r in range(hours + 1, hours + 3):
+        everything = everything + total[r : r + 1, :]
+    mean = jnp.where(row_id < hours, total / everything, 0.0)
+    duals[...] = mult_ref[...]
+    numerators = []
+    for i in range(ITERS):
+        average = mean[:, :gens]
         for o in range(1, areas):
             ecopy(i, o).wait_recv()
-        received = dot(ebuf[i, 0], sel[:nports, :])
+        top = rows if i == 0 else rows + hp
+        received = dot(ebuf[i, 0, :top, :], sel[:nports, :])
         for b in range(1, areas):
-            received = received + dot(ebuf[i, b], sel[b * nports : (b + 1) * nports, :])
+            received = received + dot(
+                ebuf[i, b, :top, :], sel[b * nports : (b + 1) * nports, :]
+            )
+        received = received * susc
+        if i > 0:
+            if i == 1:
+                still_mean = get_sums(1) / everything
+            source = jnp.concatenate((received[rows:], pen * average), axis=1)
+            mean = still_mean + apply(source)
+            average = mean[:, :gens]
+            duals[...] = duals[...] + pen * (dispatch - over_scenarios(average))
+        if i == ITERS - 1:
+            ebuf[ITERS, area, rows:, :] = mean[:, gens:].astype(jnp.bfloat16)
+            send_exchange(ITERS)
         hedge = over_scenarios(pen * average) - duals[...]
-        return jnp.concatenate((received * susc, hedge), axis=1)
-
-    spreads = []
-    average, spread = get_mean(0)
-    spreads.append(spread)
-    for i in range(ITERS):
-        source = gather(i, average)
-        high, low = split(source)
-        update = base + dot(high, hsub[...]) + dot(low, hsub[...])
+        source = jnp.concatenate((received[:rows], hedge), axis=1)
+        update = base + apply(source)
+        previous, dispatch = dispatch, update[:, :gens]
         if i < ITERS - 1:
-            send_ports(i + 1, update[:, gens:])
-        dispatch = update[:, :gens]
-        send_mean(i + 1, dispatch)
-        if i == ITERS - 1:
-            sol_ref[:, :gens] = dispatch
-            for j in range(gens // BLOCK, blocks):
-                cols = slice(j * BLOCK, (j + 1) * BLOCK)
-                sol_ref[:, cols] = full[:, cols] + dot(high, h[:, cols]) + dot(low, h[:, cols])
-        average, spread = get_mean(i + 1)
-        spreads.append(spread)
-        duals[...] = duals[...] + pen * (dispatch - over_scenarios(average))
-
-    newm_ref[...] = duals[...]
-    cons_ref[...] = average
-    lane = iota(spread_ref.shape, 1)
-    line = jnp.zeros(spread_ref.shape, jnp.float32)
-    for i, spread in enumerate(spreads):
-        line = jnp.where(lane == i, spread, line)
-    spread_ref[...] = line
-
-    for i in range(ITERS):
+            ebuf[i + 1, area, :rows, :] = update[:, gens:].astype(jnp.bfloat16)
+            ebuf[i + 1, area, rows:, :] = mean[:, gens:].astype(jnp.bfloat16)
+            send_exchange(i + 1)
+        numerators.append(squares(previous, average))
+
+    numerators.append(squares(dispatch, average))
+    lane = iota(qbuf.shape[1:], 1)
+    line = jnp.zeros(qbuf.shape[1:], jnp.float32)
+    for i, value in enumerate(numerators):
+        line = jnp.where(lane == i, value, line)
+    qbuf[group] = line
+    for o in range(1, groups):
+        qcopy(o).start()
+
+    high, low = split(source)
+    sol_ref[:, :gens] = dispatch
+    for j in range(gens // BLOCK, blocks):
+        cols = slice(j * BLOCK, (j + 1) * BLOCK)
+        sol_ref[:, cols] = full[:, cols] + dot(high, h[:, cols]) + dot(low, h[:, cols])
+
+    for o in range(1, areas):
+        ecopy(ITERS, o).wait_recv()
+    received = dot(ebuf[ITERS, 0, rows:, :], sel[:nports, :])
+    for b in range(1, areas):
+        received = received + dot(
+            ebuf[ITERS, b, rows:, :], sel[b * nports : (b + 1) * nports, :]
+        )
+    source = jnp.concatenate((received * susc, pen * average), axis=1)
+    last = (still_mean + apply(source))[:, :gens]
+    newm_ref[...] = duals[...] + pen * (dispatch - over_scenarios(last))
+    cons_ref[...] = last[:hours]
+    for o in range(1, groups):
+        qcopy(o).wait_recv()
+    line = qbuf[0]
+    for g in range(1, groups):
+        line = line + qbuf[g]
+    step = (last - average)[:hours]
+    line = line[:1, : ITERS + 1] / everything[:, : ITERS + 1]
+    line = jnp.where(iota(line.shape, 1) == ITERS, line - jnp.sum(step * step), line)
+    spread_ref[...] = line / (hours * gens)
+
+    for i in range(ITERS + 1):
         for o in range(1, areas):
             ecopy(i, o).wait_send()
-    for i in range(ITERS + 1):
-        for o in range(1, groups):
+    for o in range(1, groups):
+        for i in range(2):
             pcopy(i, o).wait_send()
+        qcopy(o).wait_send()
 
 
 def store(*refs):
@@ -282,7 +356,7 @@
     ports, _, _, local_bus, _ = tables
     nports = ports.shape[1]
     width = local_bus.shape[1] * local_bus.shape[2]
-    hp = -(-(hours + 2) // 8) * 8
+    hp = -(-(hours + 3) // 16) * 16
     inner = width + gens
     bf, f32 = jnp.bfloat16, jnp.float32
     vmem = pl.BlockSpec(memory_space=pltpu.VMEM)
@@ -296,8 +370,8 @@
             jax.ShapeDtypeStruct((1, ITERS + 1), f32),
         ),
         in_specs=[
-            vmem,
-            vmem,
+            pl.BlockSpec(memory_space=pl.ANY),
+            pl.BlockSpec(memory_space=pl.ANY),
             vmem,
             pl.BlockSpec(memory_space=pltpu.SMEM),
             vmem,
@@ -307,6 +381,8 @@
         out_specs=(vmem,) * 4,
         scratch_shapes=[
             pltpu.VMEM((buses, buses), bf),
+            pltpu.VMEM((rows, buses), f32),
+            pltpu.VMEM((rows, buses), f32),
             pltpu.VMEM((rows + width, buses), bf),
             pltpu.VMEM((rows, buses), f32),
             pltpu.VMEM((inner, buses), bf),
@@ -315,13 +391,17 @@
             pltpu.VMEM((2 * rows + inner, nports), f32),
             pltpu.VMEM((inner, gens + nports), bf),
             pltpu.VMEM((rows, gens), f32),
-            pltpu.VMEM((ITERS, areas, rows, nports), bf),
-            pltpu.VMEM((ITERS + 1, groups, hp, gens), f32),
+            pltpu.VMEM((ITERS + 1, areas, rows + hp, nports), bf),
+            pltpu.VMEM((2, groups, hp, gens + nports), bf),
+            pltpu.VMEM((groups, 8, 128), f32),
             dma((buses // BLOCK,)),
-            dma((ITERS, areas)),
-            dma((ITERS, areas)),
-            dma((ITERS + 1, groups)),
-            dma((ITERS + 1, groups)),
+            dma((2,)),
+            dma((ITERS + 1, areas)),
+            dma((ITERS + 1, areas)),
+            dma((2, groups)),
+            dma((2, groups)),
+            dma((groups,)),
+            dma((groups,)),
         ],
         compiler_params=pltpu.CompilerParams(collective_id=0, has_side_effects=True),
         name="hedging",

time: 38.5 us -> 36.6 us (0.951)
  Pallas kernels: 37.7 us -> 35.8 us
    pallas_call x1, Pallas kernels: 35.6 us -> 33.6 us  [shards(): pl.pallas_call(functools.partial(kernel, areas, groups), out_shape=(jax.S...]
where the time goes in v3:
time: 36.6 us; the launch traced here: 36.4 us
  Pallas kernels  35.8 us (98%)
  between operations  0.64 us (2%)
    pallas_call x1, Pallas kernels, shards(): pl.pallas_call(functools.partial(kernel, areas, groups), out_shape=(jax.S...  33.6 us
    pallas_call x1, Pallas kernels, shards(): pl.pallas_call(store, out_shape=tuple((jax.ShapeDtypeStruct(x.shape, x.dt...  2.13 us

profile of v3, /device:TPU:0, one launch (start us, length us, event | category | flops | bytes accessed | tf_op | source)
XLA Modules:
  0.0 36.4 jit_solution(14813241463267994194)
XLA Ops:
  0.6 33.6 %hedging.1 = (f32[96,2048]{1,0:T(8,128)}, f32[96,256]{1,0:T(8,128)}, f32[12,256]{1,0:T(8,128)}, f32[1,5]{1,0:T(1,128)}) custom-call(f32[96,2048]{1,0:T(8,128)} %bitcast.16, f32[96,2048]{1,0:T(8,128)} %bitcast.17, f32[96,256]{1,0:T(8,128)} %bitcast.18, f32[8]{0:T(128)} %weight_ref.1, f32[1,256]{1,0:T(1,128)} %bitcast.19, bf16[2048,2048]{1,0:T(8,128)(2,1)} %inv_ref.1, ...), custom_call_target="tpu_custom_call" | custom-call | tf_op jit(solution)/shard_map/hedging/pallas_call | solution.py:364
  34.3 2.1 %store.1 = (f32[96,2048]{1,0:T(8,128)}, f32[96,256]{1,0:T(8,128)}, f32[12,256]{1,0:T(8,128)}, f32[1,5]{1,0:T(1,128)}) custom-call(f32[96,2048]{1,0:T(8,128)} %get-tuple-element.12.refs_0_, f32[96,256]{1,0:T(8,128)} %get-tuple-element.13.refs_1_, f32[12,256]{1,0:T(8,128)} %get-tuple-element.14.refs_2_, f32[1,5]{1,0:T(1,128)} %get-tuple-element.15.refs_3_), custom_call_target="tpu_custom_call" | custom-call | tf_op jit(solution)/shard_map/store/pallas_call | solution.py:409

commit v4 on v3

--- a/solution.py
+++ b/solution.py
@@ -22,7 +22,13 @@
 
 
 def exact(a, b):
-    return jnp.dot(a, b, precision=lax.Precision.HIGHEST, preferred_element_type=jnp.float32)
+    total = jnp.zeros((a.shape[0], b.shape[1]), jnp.float32)
+    rest, other, first = (b, a, False) if a.shape[1] == b.shape[0] and a.shape[0] > b.shape[1] else (a, b, True)
+    for _ in range(3):
+        piece = rest.astype(jnp.bfloat16)
+        rest = rest - piece.astype(jnp.float32)
+        total = total + (dot(piece, other.astype(jnp.bfloat16)) if first else dot(other.astype(jnp.bfloat16), piece))
+    return total
 
 
 def iota(shape, axis):
@@ -43,11 +49,12 @@
     rport_ref,
     lbus_ref,
     susc_ref,
-    sol_ref,
+    sol_hbm,
     newm_ref,
     cons_ref,
     spread_ref,
     inv,
+    sol_ref,
     load_ref,
     start_ref,
     left,
@@ -62,6 +69,7 @@
     pbuf,
     qbuf,
     dma_sem,
+    out_sem,
     in_sem,
     esend,
     erecv,
@@ -151,7 +159,7 @@
     row_id = iota((hp, inside), 0)
 
     def over_scenarios(x):
-        return jnp.broadcast_to(x[:hours, None, :], (hours, scen, gens)).reshape(rows, gens)
+        return jnp.broadcast_to(x[:hours, None, :], (hours, scen, x.shape[1])).reshape(rows, x.shape[1])
 
     def send_sums(i, x):
         sums = jnp.sum(weights[None] * x.reshape(hours, scen, inside), axis=1)
@@ -245,12 +253,23 @@
     )
     pen = pen_ref[...]
 
-    def apply(source):
+    def through(source, first, count):
         high, low = split(source)
-        return dot(high, hsub[...]) + dot(low, hsub[...])
-
-    high, low = split(mult_ref[...])
-    still = base - dot(high, hsub[width:, :]) - dot(low, hsub[width:, :])
+        part = hsub[first : first + count, :]
+        return dot(high, part) + dot(low, part)
+
+    def arrived(i, first, count):
+        for o in range(1, areas):
+            ecopy(i, o).wait_recv()
+        received = dot(ebuf[i, 0, first : first + count, :], sel[:nports, :])
+        for b in range(1, areas):
+            received = received + dot(
+                ebuf[i, b, first : first + count, :], sel[b * nports : (b + 1) * nports, :]
+            )
+        received = received * susc
+        return received, dot(received.astype(jnp.bfloat16), hsub[:width, :])
+
+    still = base - through(mult_ref[...], width, gens)
     send_sums(1, still)
     total = get_sums(0)
     everything = total[hours : hours + 1, :]
@@ -259,36 +278,29 @@
     mean = jnp.where(row_id < hours, total / everything, 0.0)
     duals[...] = mult_ref[...]
     numerators = []
+    before = still
     for i in range(ITERS):
-        average = mean[:, :gens]
-        for o in range(1, areas):
-            ecopy(i, o).wait_recv()
-        top = rows if i == 0 else rows + hp
-        received = dot(ebuf[i, 0, :top, :], sel[:nports, :])
-        for b in range(1, areas):
-            received = received + dot(
-                ebuf[i, b, :top, :], sel[b * nports : (b + 1) * nports, :]
-            )
-        received = received * susc
+        received, added = arrived(i, 0, rows if i == 0 else rows + hp)
         if i > 0:
             if i == 1:
                 still_mean = get_sums(1) / everything
-            source = jnp.concatenate((received[rows:], pen * average), axis=1)
-            mean = still_mean + apply(source)
-            average = mean[:, :gens]
-            duals[...] = duals[...] + pen * (dispatch - over_scenarios(average))
+            mean = still_mean + pull + added[rows:]
+        average = mean[:, :gens]
         if i == ITERS - 1:
             ebuf[ITERS, area, rows:, :] = mean[:, gens:].astype(jnp.bfloat16)
             send_exchange(ITERS)
-        hedge = over_scenarios(pen * average) - duals[...]
-        source = jnp.concatenate((received[:rows], hedge), axis=1)
-        update = base + apply(source)
+        pull = through(pen * average, width, gens)
+        update = before + added[:rows] + over_scenarios(pull if i == 0 else pull + pull)
         previous, dispatch = dispatch, update[:, :gens]
         if i < ITERS - 1:
             ebuf[i + 1, area, :rows, :] = update[:, gens:].astype(jnp.bfloat16)
             ebuf[i + 1, area, rows:, :] = mean[:, gens:].astype(jnp.bfloat16)
             send_exchange(i + 1)
+        if i > 0:
+            duals[...] = duals[...] + pen * (previous - over_scenarios(average))
         numerators.append(squares(previous, average))
+        if i < ITERS - 1:
+            before = base - through(duals[...] + pen * dispatch, width, gens)
 
     numerators.append(squares(dispatch, average))
     lane = iota(qbuf.shape[1:], 1)
@@ -299,21 +311,18 @@
     for o in range(1, groups):
         qcopy(o).start()
 
-    high, low = split(source)
+    hedge = over_scenarios(pen * average) - duals[...]
+    high = jnp.concatenate((received[:rows], hedge), axis=1).astype(jnp.bfloat16)
     sol_ref[:, :gens] = dispatch
     for j in range(gens // BLOCK, blocks):
         cols = slice(j * BLOCK, (j + 1) * BLOCK)
-        sol_ref[:, cols] = full[:, cols] + dot(high, h[:, cols]) + dot(low, h[:, cols])
-
-    for o in range(1, areas):
-        ecopy(ITERS, o).wait_recv()
-    received = dot(ebuf[ITERS, 0, rows:, :], sel[:nports, :])
-    for b in range(1, areas):
-        received = received + dot(
-            ebuf[ITERS, b, rows:, :], sel[b * nports : (b + 1) * nports, :]
-        )
-    source = jnp.concatenate((received * susc, pen * average), axis=1)
-    last = (still_mean + apply(source))[:, :gens]
+        sol_ref[:, cols] = full[:, cols] + dot(high, h[:, cols])
+
+    solved = pltpu.make_async_copy(sol_ref, sol_hbm, out_sem)
+    solved.start()
+
+    _, added = arrived(ITERS, rows, hp)
+    last = (still_mean + pull + added)[:, :gens]
     newm_ref[...] = duals[...] + pen * (dispatch - over_scenarios(last))
     cons_ref[...] = last[:hours]
     for o in range(1, groups):
@@ -326,6 +335,7 @@
     line = jnp.where(iota(line.shape, 1) == ITERS, line - jnp.sum(step * step), line)
     spread_ref[...] = line / (hours * gens)
 
+    solved.wait()
     for i in range(ITERS + 1):
         for o in range(1, areas):
             ecopy(i, o).wait_send()
@@ -378,9 +388,10 @@
             pl.BlockSpec(memory_space=pl.ANY),
         ]
         + [vmem] * 5,
-        out_specs=(vmem,) * 4,
+        out_specs=(pl.BlockSpec(memory_space=pl.ANY),) + (vmem,) * 3,
         scratch_shapes=[
             pltpu.VMEM((buses, buses), bf),
+            pltpu.VMEM((rows, buses), f32),
             pltpu.VMEM((rows, buses), f32),
             pltpu.VMEM((rows, buses), f32),
             pltpu.VMEM((rows + width, buses), bf),
@@ -395,6 +406,7 @@
             pltpu.VMEM((2, groups, hp, gens + nports), bf),
             pltpu.VMEM((groups, 8, 128), f32),
             dma((buses // BLOCK,)),
+            dma,
             dma((2,)),
             dma((ITERS + 1, areas)),
             dma((ITERS + 1, areas)),

time: 36.6 us -> 35.9 us (0.981)
  Pallas kernels: 35.8 us -> 35.1 us
    pallas_call x1, Pallas kernels: 33.6 us -> 33 us  [shards(): pl.pallas_call(functools.partial(kernel, areas, groups), out_shape=(jax.S...]
where the time goes in v4:
time: 35.9 us; the launch traced here: 35.7 us
  Pallas kernels  35.1 us (98%)
  between operations  0.64 us (2%)
    pallas_call x1, Pallas kernels, shards(): pl.pallas_call(functools.partial(kernel, areas, groups), out_shape=(jax.S...  33 us
    pallas_call x1, Pallas kernels, shards(): pl.pallas_call(store, out_shape=tuple((jax.ShapeDtypeStruct(x.shape, x.dt...  2.13 us

profile of v4, /device:TPU:0, one launch (start us, length us, event | category | flops | bytes accessed | tf_op | source)
XLA Modules:
  0.0 35.7 jit_solution(5378932486149297140)
XLA Ops:
  0.6 33.0 %hedging.1 = (f32[96,2048]{1,0:T(8,128)}, f32[96,256]{1,0:T(8,128)}, f32[12,256]{1,0:T(8,128)}, f32[1,5]{1,0:T(1,128)}) custom-call(f32[96,2048]{1,0:T(8,128)} %bitcast.16, f32[96,2048]{1,0:T(8,128)} %bitcast.17, f32[96,256]{1,0:T(8,128)} %bitcast.18, f32[8]{0:T(128)} %weight_ref.1, f32[1,256]{1,0:T(1,128)} %bitcast.19, bf16[2048,2048]{1,0:T(8,128)(2,1)} %inv_ref.1, ...), custom_call_target="tpu_custom_call" | custom-call | tf_op jit(solution)/shard_map/hedging/pallas_call | solution.py:374
  33.6 2.1 %store.1 = (f32[96,2048]{1,0:T(8,128)}, f32[96,256]{1,0:T(8,128)}, f32[12,256]{1,0:T(8,128)}, f32[1,5]{1,0:T(1,128)}) custom-call(f32[96,2048]{1,0:T(8,128)} %get-tuple-element.12.refs_0_, f32[96,256]{1,0:T(8,128)} %get-tuple-element.13.refs_1_, f32[12,256]{1,0:T(8,128)} %get-tuple-element.14.refs_2_, f32[1,5]{1,0:T(1,128)} %get-tuple-element.15.refs_3_), custom_call_target="tpu_custom_call" | custom-call | tf_op jit(solution)/shard_map/store/pallas_call | solution.py:421

commit v5 on v4

--- a/solution.py
+++ b/solution.py
@@ -94,13 +94,6 @@
         cols = pl.ds(pl.multiple_of(j * BLOCK, BLOCK), BLOCK)
         return pltpu.make_async_copy(inv_ref.at[:, cols], inv.at[:, cols], dma_sem.at[j])
 
-    load_in = pltpu.make_async_copy(load_hbm, load_ref, in_sem.at[0])
-    start_in = pltpu.make_async_copy(start_hbm, start_ref, in_sem.at[1])
-    start_in.start()
-    load_in.start()
-    for j in range(blocks):
-        fetch(j).start()
-
     barrier = pltpu.get_barrier_semaphore()
     for o in range(1, areas):
         pl.semaphore_signal(
@@ -116,6 +109,13 @@
             device_id={"scen": lax.rem(group + o, groups)},
             device_id_type=pl.DeviceIdType.MESH,
         )
+
+    load_in = pltpu.make_async_copy(load_hbm, load_ref, in_sem.at[0])
+    start_in = pltpu.make_async_copy(start_hbm, start_ref, in_sem.at[1])
+    start_in.start()
+    load_in.start()
+    for j in range(blocks):
+        fetch(j).start()
 
     def ecopy(i, o):
         first = rows if i == ITERS else 0

time: 35.9 us -> 36 us (level)
  no operation moved by 1% of the time
where the time goes in v5:
time: 36 us; the launch traced here: 35.9 us
  Pallas kernels  35.2 us (98%)
  between operations  0.64 us (2%)
    pallas_call x1, Pallas kernels, shards(): pl.pallas_call(functools.partial(kernel, areas, groups), out_shape=(jax.S...  33.1 us
    pallas_call x1, Pallas kernels, shards(): pl.pallas_call(store, out_shape=tuple((jax.ShapeDtypeStruct(x.shape, x.dt...  2.13 us

profile of v5, /device:TPU:0, one launch (start us, length us, event | category | flops | bytes accessed | tf_op | source)
XLA Modules:
  0.0 35.9 jit_solution(7166194695000549935)
XLA Ops:
  0.6 33.1 %hedging.1 = (f32[96,2048]{1,0:T(8,128)}, f32[96,256]{1,0:T(8,128)}, f32[12,256]{1,0:T(8,128)}, f32[1,5]{1,0:T(1,128)}) custom-call(f32[96,2048]{1,0:T(8,128)} %bitcast.16, f32[96,2048]{1,0:T(8,128)} %bitcast.17, f32[96,256]{1,0:T(8,128)} %bitcast.18, f32[8]{0:T(128)} %weight_ref.1, f32[1,256]{1,0:T(1,128)} %bitcast.19, bf16[2048,2048]{1,0:T(8,128)(2,1)} %inv_ref.1, ...), custom_call_target="tpu_custom_call" | custom-call | tf_op jit(solution)/shard_map/hedging/pallas_call | solution.py:374
  33.7 2.1 %store.1 = (f32[96,2048]{1,0:T(8,128)}, f32[96,256]{1,0:T(8,128)}, f32[12,256]{1,0:T(8,128)}, f32[1,5]{1,0:T(1,128)}) custom-call(f32[96,2048]{1,0:T(8,128)} %get-tuple-element.12.refs_0_, f32[96,256]{1,0:T(8,128)} %get-tuple-element.13.refs_1_, f32[12,256]{1,0:T(8,128)} %get-tuple-element.14.refs_2_, f32[1,5]{1,0:T(1,128)} %get-tuple-element.15.refs_3_), custom_call_target="tpu_custom_call" | custom-call | tf_op jit(solution)/shard_map/store/pallas_call | solution.py:421
